TPU v7x, 512 devices: a whole 4x4x16 slice. The times are simulated.
512 devices in a mesh: row: 16 (over y, x), col: 32 (over z, core).
Axes of the slice: x: 4, y: 4, z: 16, core: 2. Of those that a mesh axis runs over, the one named last changes fastest.
Arguments:
- out_grad: bfloat16 [2048, 8192], P('col', 'row'), may hold values from -6 to 6
- hidden: bfloat16 [2048, 28672], P('row', 'col'), may hold values from -0.12988281 to 0.12988281
- weight: bfloat16 [28672, 8192], P('col', 'row'), may hold values from -0.03125 to 0.03125
Outputs:
- token_grad: bfloat16 [2048, 28672], P('row', 'col')
- weight_grad: bfloat16 [28672, 8192], P('col', 'row')
All inputs are finite; a program needn't handle non-finite values.
Results may differ from a plain program's by a relative error of at most 0.001.
Values may be sent and summed in bfloat16 or wider, within the bound.
A program may use at most 64 MiB of HBM per device.

v0:
```python
import jax
import jax.numpy as jnp
from jax import lax
from jax.sharding import PartitionSpec as P


def on_device(out_grad, hidden, weight):
    gathered = lax.all_gather(out_grad, "col", axis=0, tiled=True)
    cotangent = gathered
    weight_sum = lax.dot_general(
        lax.all_gather(hidden, "row", axis=0, tiled=True),
        cotangent,
        (((0,), (0,)), ((), ())),
        preferred_element_type=jnp.float32,
    )
    weight_grad = weight_sum.astype(jnp.bfloat16)
    own_full = lax.all_to_all(gathered, "row", split_axis=0, concat_axis=1, tiled=True)
    cotangent = own_full
    token_sum = lax.dot_general(
        cotangent,
        lax.all_gather(weight, "row", axis=1, tiled=True),
        (((1,), (1,)), ((), ())),
        preferred_element_type=jnp.float32,
    )
    return (token_sum.astype(jnp.bfloat16), weight_grad)


def solution(mesh):
    return jax.shard_map(
        on_device,
        mesh=mesh,
        in_specs=(P("col", "row"), P("row", "col"), P("col", "row")),
        out_specs=(P("row", "col"), P("col", "row")),
        check_vma=False,
    )
```

profile of v0, /device:TPU:1, one launch (start us, length us, event | category | flops | bytes accessed | tf_op | source)
XLA Modules:
  0.0 301.2 jit_solution(12447496459693819890)
XLA Ops:
  7.2 0.0 all-gather.4.cloned.1.call-start
  7.2 0.7 all-gather.4.cloned.1.call-update
  7.9 0.0 all-gather.8.cloned.1.call-start
  7.9 0.7 all-gather.8.cloned.1.call-update
  8.6 0.0 all-gather.6.cloned.1.call-start
  8.7 0.7 all-gather.6.cloned.1.call-update
  9.4 78.3 %all-gather.4.cloned.1.call-done = bf16[2048,512]{1,0:T(8,128)(2,1)} async-done(((bf16[64,512]{1,0:T(8,128)(2,1)}), bf16[2048,512]{1,0:T(8,128)(2,1)}) %all-gather.4.cloned.1.call-update) | async-done | bytes 2097168 | tf_op jit(solution)/shard_map/all_gather | solution.py:8
  87.7 37.9 %all_to_all.19 = bf16[16,128,512]{2,1,0:T(8,128)(2,1)S(1)} all-to-all(bf16[16,128,512]{2,1,0:T(8,128)(2,1)} %bitcast.9), channel_id=1, replica_groups=mesh['row'=16,'col'=32] {'row'}, dimensions={0} | all-to-all | bytes 4194304 | tf_op jit(solution)/shard_map/all_to_all | solution.py:17
  125.6 2.4 copy.5
  127.9 0.0 copy-start
  127.9 28.6 %all-gather.8.cloned.1.call-done = bf16[2048,896]{1,0:T(8,128)(2,1)} async-done(((bf16[128,896]{1,0:T(8,128)(2,1)}), bf16[2048,896]{1,0:T(8,128)(2,1)}) %all-gather.8.cloned.1.call-update) | async-done | bytes 3670032 | tf_op jit(solution)/shard_map/all_gather | solution.py:11
  156.6 5.7 %convolution_convert_fusion = bf16[896,512]{1,0:T(8,128)(2,1)} fusion(bf16[2048,896]{1,0:T(8,128)(2,1)} %all-gather.8.cloned.1.call-done, bf16[2048,512]{1,0:T(8,128)(2,1)} %all-gather.4.cloned.1.call-done), kind=kOutput, calls=%fused_computation | convolution fusion | flops 1879506944 | bytes 6684672 | tf_op jit(solution)/shard_map/dot_general | solution.py:10
  162.3 121.8 %all-gather.6.cloned.1.call-done = bf16[896,8192]{1,0:T(8,128)(2,1)} async-done(((bf16[896,512]{1,0:T(8,128)(2,1)}), bf16[896,8192]{1,0:T(8,128)(2,1)}) %all-gather.6.cloned.1.call-update) | async-done | bytes 14680080 | tf_op jit(solution)/shard_map/all_gather | solution.py:21
  284.1 0.0 copy-done
  284.1 10.6 %convolution_convert_fusion.1 = bf16[128,896]{1,0:T(8,128)(2,1)} fusion(bf16[128,8192]{0,1:T(8,128)(2,1)S(1)} %bitcast.8, bf16[896,8192]{1,0:T(8,128)(2,1)} %all-gather.6.cloned.1.call-done), kind=kOutput, calls=%fused_computation.1 | convolution fusion | flops 1879162880 | bytes 17006592 | tf_op jit(solution)/shard_map/dot_general | solution.py:19
Async XLA Ops:
  7.2 80.5 %all-gather.4.cloned.1.call-start = ((), (), s32[]{:S(2)}) async-start(), calls=%async_computation.1 | async-start | bytes 2162688 | tf_op jit(solution)/shard_map/all_gather | solution.py:8
  7.9 148.7 %all-gather.8.cloned.1.call-start = ((), (), s32[]{:S(2)}) async-start(), calls=%async_computation.3 | async-start | bytes 3899392 | tf_op jit(solution)/shard_map/all_gather | solution.py:11
  8.6 275.4 %all-gather.6.cloned.1.call-start = ((), (), s32[]{:S(2)}) async-start(), calls=%async_computation.2 | async-start | bytes 15597568 | tf_op jit(solution)/shard_map/all_gather | solution.py:21
  127.9 156.1 %copy-start = (bf16[128,16,512]{0,2,1:T(8,128)(2,1)S(1)}, bf16[128,16,512]{0,2,1:T(8,128)(2,1)}, u32[]{:S(2)}) copy-start(bf16[128,16,512]{0,2,1:T(8,128)(2,1)} %copy.5) | copy-start | bytes 6291460
Sparse Core Ops, SparseCore 0:
  10.1 77.5 all-gather.3
  90.7 65.8 all-gather.7
  159.6 124.4 all-gather.5
where the time goes:
time: 301 us
  waiting for transfers between devices  231 us (77%)
  blocking collectives  37.9 us (13%)
  matrix products  16.3 us (5%)
  between operations  13.7 us (5%)
    all_gather x1, waiting for transfers between devices, on_device(): lax.all_gather(weight, 'row', axis=1, tiled=True)  122 us
    all_gather x1, waiting for transfers between devices, on_device(): gathered = lax.all_gather(out_grad, 'col', axis=0, tiled=True)  78.3 us
    all_to_all x1, blocking collectives, on_device(): lax.all_to_all(gathered, 'row', split_axis=0, concat_axis=1, tiled=True)  37.9 us
    all_gather x1, waiting for transfers between devices, on_device(): lax.all_gather(hidden, 'row', axis=0, tiled=True)  28.6 us
    dot_general x1, matrix products, on_device(): lax.dot_general(cotangent, lax.all_gather(weight, 'row', axis=1, tiled=Tr...  10.6 us
  transfers between devices with their start and end apart: 3, of which 3 were waited for; matrix products, arithmetic and copies ran while one was open for 3% of the time, Pallas kernels for 0%

commit v1 on v0

--- a/solution.py
+++ b/solution.py
@@ -5,10 +5,19 @@
 
 
 def on_device(out_grad, hidden, weight):
+
+    def handle_surface_now(patch, across):
+        return jnp.concatenate(
+            lax.all_to_all(
+                jnp.stack([patch for _ in range(lax.axis_size(across))], axis=0), across, 0, 0
+            ),
+            axis=0,
+        )
+
     gathered = lax.all_gather(out_grad, "col", axis=0, tiled=True)
     cotangent = gathered
     weight_sum = lax.dot_general(
-        lax.all_gather(hidden, "row", axis=0, tiled=True),
+        handle_surface_now(hidden, "row"),
         cotangent,
         (((0,), (0,)), ((), ())),
         preferred_element_type=jnp.float32,

time: 301 us -> 239 us (0.79)
  waiting for transfers between devices: 231 us -> 147 us
  blocking collectives: 37.9 us -> 50.3 us
  starting transfers between devices: 0.11 us -> 6.76 us
    all_gather x1, waiting for transfers between devices: 78.3 us -> 27.1 us  [on_device(): gathered = lax.all_gather(out_grad, 'col', axis=0, tiled=True)]
    all_gather x1, waiting for transfers between devices: 122 us -> 86.1 us  [on_device(): lax.all_gather(weight, 'row', axis=1, tiled=True)]
    all_to_all x0 -> x1, waiting for transfers between devices: none -> 32 us  [on_device(): lax.all_to_all(gathered, 'row', split_axis=0, concat_axis=1, tiled=True)]
    all_gather x1 -> x0, waiting for transfers between devices: 28.6 us -> none  [on_device(): lax.all_gather(hidden, 'row', axis=0, tiled=True)]
    all_to_all x1, blocking collectives: 37.9 us -> 50.3 us  [handle_surface_now(): lax.all_to_all(jnp.stack([patch for _ in range(lax.axis_size(across))], a...]
    all_to_all x0 -> x1, starting transfers between devices: none -> 6.69 us  [on_device(): lax.all_to_all(gathered, 'row', split_axis=0, concat_axis=1, tiled=True)]
  transfers between devices with their start and end apart: 3 -> 3, of which waited for: 3 -> 3; matrix products, arithmetic and copies ran while one was open for 3% -> 4% of each run, Pallas kernels for 0% -> 0%
where the time goes in v1:
time: 239 us; the launch traced here: 238 us
  waiting for transfers between devices  147 us (62%)
  blocking collectives  50.3 us (21%)
  matrix products  16.9 us (7%)
  between operations  14.1 us (6%)
  starting transfers between devices  6.76 us (3%)
  local copies, waits for them, and re-layouts  3.81 us (2%)
    all_gather x1, waiting for transfers between devices, on_device(): lax.all_gather(weight, 'row', axis=1, tiled=True)  86.1 us
    all_to_all x1, blocking collectives, handle_surface_now(): lax.all_to_all(jnp.stack([patch for _ in range(lax.axis_size(across))], a...  50.3 us
    all_to_all x1, waiting for transfers between devices, on_device(): lax.all_to_all(gathered, 'row', split_axis=0, concat_axis=1, tiled=True)  32 us
    all_gather x1, waiting for transfers between devices, on_device(): gathered = lax.all_gather(out_grad, 'col', axis=0, tiled=True)  27.1 us
    dot_general x1, matrix products, on_device(): lax.dot_general(cotangent, lax.all_gather(weight, 'row', axis=1, tiled=Tr...  11.2 us
    all_to_all x1, starting transfers between devices, on_device(): lax.all_to_all(gathered, 'row', split_axis=0, concat_axis=1, tiled=True)  6.69 us
    dot_general x1, matrix products, on_device(): lax.dot_general(handle_surface_now(hidden, 'row'), cotangent, (((0,), (0,...  5.72 us
  transfers between devices with their start and end apart: 3, of which 3 were waited for; matrix products, arithmetic and copies ran while one was open for 4% of the time, Pallas kernels for 0%

profile of v1, /device:TPU:1, one launch (start us, length us, event | category | flops | bytes accessed | tf_op | source)
XLA Modules:
  0.0 238.4 jit_solution(16517772892827461739)
XLA Ops:
  7.2 0.0 all-gather.3.cloned.1.call-start
  7.2 0.7 all-gather.3.cloned.1.call-update
  7.9 0.0 all-gather.5.cloned.1.call-start
  7.9 0.7 all-gather.5.cloned.1.call-update
  8.6 1.4 stack.2
  10.1 50.3 %all_to_all.24 = bf16[16,128,896]{2,1,0:T(8,128)(2,1)} all-to-all(bf16[16,128,896]{2,1,0:T(8,128)(2,1)S(1)} %stack.2), channel_id=1, replica_groups=mesh['row'=16,'col'=32] {'row'}, dimensions={0} | all-to-all | bytes 7340032 | tf_op jit(solution)/shard_map/all_to_all | solution.py:11
  60.4 27.1 %all-gather.3.cloned.1.call-done = bf16[2048,512]{1,0:T(8,128)(2,1)} async-done(((bf16[64,512]{1,0:T(8,128)(2,1)}), bf16[2048,512]{1,0:T(8,128)(2,1)}) %all-gather.3.cloned.1.call-update) | async-done | bytes 2097168 | tf_op jit(solution)/shard_map/all_gather | solution.py:17
  87.4 6.7 %all-to-all-start = ((bf16[16,128,512]{2,1,0:T(8,128)(2,1)}), bf16[16,128,512]{2,1,0:T(8,128)(2,1)S(1)}, u32[]{:S(2)}, u32[]{:S(2)}) async-start(bf16[16,128,512]{2,1,0:T(8,128)(2,1)} %bitcast.11), calls=%async_computation | async-start | bytes 4194304 | tf_op jit(solution)/shard_map/all_to_all | solution.py:26
  94.1 5.7 %convolution_convert_fusion = bf16[896,512]{1,0:T(8,128)(2,1)} fusion(bf16[2048,896]{1,0:T(8,128)(2,1)} %bitcast.10, bf16[2048,512]{1,0:T(8,128)(2,1)} %all-gather.3.cloned.1.call-done), kind=kOutput, calls=%fused_computation | convolution fusion | flops 1879506944 | bytes 6684672 | tf_op jit(solution)/shard_map/dot_general | solution.py:19
  99.9 32.0 %all-to-all-done = bf16[16,128,512]{2,1,0:T(8,128)(2,1)S(1)} async-done(((bf16[16,128,512]{2,1,0:T(8,128)(2,1)}), bf16[16,128,512]{2,1,0:T(8,128)(2,1)S(1)}, u32[]{:S(2)}, u32[]{:S(2)}) %all-to-all-start) | async-done | bytes 2097184 | tf_op jit(solution)/shard_map/all_to_all | solution.py:26
  131.9 2.4 copy.5
  134.2 86.1 %all-gather.5.cloned.1.call-done = bf16[896,8192]{1,0:T(8,128)(2,1)} async-done(((bf16[896,512]{1,0:T(8,128)(2,1)}), bf16[896,8192]{1,0:T(8,128)(2,1)}) %all-gather.5.cloned.1.call-update) | async-done | bytes 14680080 | tf_op jit(solution)/shard_map/all_gather | solution.py:30
  220.3 11.2 %convolution_convert_fusion.1 = bf16[128,896]{1,0:T(8,128)(2,1)} fusion(bf16[128,8192]{0,1:T(8,128)(2,1)} %bitcast.9, bf16[896,8192]{1,0:T(8,128)(2,1)} %all-gather.5.cloned.1.call-done), kind=kOutput, calls=%fused_computation.1 | convolution fusion | flops 1879162880 | bytes 17006592 | tf_op jit(solution)/shard_map/dot_general | solution.py:28
Async XLA Ops:
  7.2 80.3 %all-gather.3.cloned.1.call-start = ((), (), s32[]{:S(2)}) async-start(), calls=%async_computation.2 | async-start | bytes 2162688 | tf_op jit(solution)/shard_map/all_gather | solution.py:17
  7.9 212.4 %all-gather.5.cloned.1.call-start = ((), (), s32[]{:S(2)}) async-start(), calls=%async_computation.3 | async-start | bytes 15597568 | tf_op jit(solution)/shard_map/all_gather | solution.py:30
  87.4 44.4 %all-to-all-start = ((bf16[16,128,512]{2,1,0:T(8,128)(2,1)}), bf16[16,128,512]{2,1,0:T(8,128)(2,1)S(1)}, u32[]{:S(2)}, u32[]{:S(2)}) async-start(bf16[16,128,512]{2,1,0:T(8,128)(2,1)} %bitcast.11), calls=%async_computation | async-start | bytes 4194304 | tf_op jit(solution)/shard_map/all_to_all | solution.py:26
Sparse Core Ops, SparseCore 0:
  10.1 77.2 all-gather.2
  90.4 129.8 all-gather.4
